TPU v7x, 32 devices: a whole 2x2x4 slice. The times are simulated.
32 devices in a mesh: row: 4 (over x, core), col: 8 (over z, y).
Axes of the slice: x: 2, y: 2, z: 4, core: 2. Of those that a mesh axis runs over, the one named last changes fastest.
Arguments:
- integrals: bfloat16 [384, 64, 4096], P(('row', 'col')), may hold values from -6 to 6
- block_list: int32 [384, 3], P(('row', 'col')), may hold values from 0 to 31, as said below
- p_slot: int32 [16], replicated, may hold values from 0 to 15, as said below
- metric: bfloat16 [16, 64, 64], P('col'), may hold values from -0.75 to 0.75
- density_panel: bfloat16 [2048, 128], P(('row', 'col')), may hold values from -0.75 to 0.75
- pattern: int32 [2048], P(('row', 'col')), may hold values 0 or 1
Outputs:
- exchange_blocks: float32 [2048, 512], P(('row', 'col'))
Inputs may be any that keep to these rules, and one draw needn't show every extreme that they name: `block_list`: rows name (mu block, nu block, auxiliary block). The 12 rows of the device at position row * 8 + col have mu blocks in row * 8 to row * 8 + 7. With owner p_slot[p] // 2, no device lists more than 2 blocks for one owner, and in every row group some owner gets exactly 2 from every device of the group. A permutation; auxiliary block p is contracted by col index p_slot[p] // 2, local slot p_slot[p] % 2.
All inputs are finite; a program needn't handle non-finite values. No bound on the sum of `pattern` on one device may be relied on, other than what follows from the above.
Results may differ from a plain program's by a relative error of at most 0.00059.
Values may be sent and summed in bfloat16 or wider, within the bound.
A program may use at most 192 MiB of HBM per device.

v0:
```python
import jax
import jax.numpy as jnp
from jax import lax
from jax.sharding import PartitionSpec as P

MB = 8
CAP = 2


def on_device(integrals, block_list, p_slot, metric, density_panel, pattern):
    columns = lax.axis_size("col")
    owned_slots = metric.shape[0]
    block_size = metric.shape[1]
    listed = integrals.shape[0]
    panel_width = density_panel.shape[1]
    total_slots = columns * CAP
    all_slots = owned_slots * columns
    row_here = lax.axis_index("row")
    first_ids = block_list[:, 0] - row_here * MB
    second_ids = block_list[:, 1]
    fitting_ids = block_list[:, 2]
    slot_match = fitting_ids[:, None] == jnp.arange(all_slots, dtype=jnp.int32)[None, :]
    slot_ids = jnp.sum(jnp.where(slot_match, p_slot[None, :], 0), axis=1)
    owners = slot_ids // owned_slots
    local_slot = slot_ids % owned_slots
    same_owner = owners[:, None] == owners[None, :]
    before = jnp.arange(listed)[None, :] < jnp.arange(listed)[:, None]
    position = jnp.sum(same_owner & before, axis=1)
    target = owners * CAP + position
    slot_hits = jnp.arange(total_slots, dtype=jnp.int32)[:, None] == target[None, :]
    placing = slot_hits.astype(jnp.bfloat16)
    outgoing = jnp.dot(
        placing, integrals.reshape(listed, -1), preferred_element_type=jnp.float32
    ).astype(jnp.bfloat16)
    outgoing = outgoing.reshape(columns, CAP, block_size, block_size * block_size)
    labels = jnp.stack([first_ids, local_slot, second_ids, jnp.ones_like(first_ids)], axis=1)
    label_send = jnp.sum(jnp.where(slot_hits[:, :, None], labels[None, :, :], 0), axis=1).astype(
        jnp.bfloat16
    )
    label_send = label_send.reshape(columns, CAP, 4)
    arrived, arrived_labels = (
        lax.all_to_all(outgoing, "col", split_axis=0, concat_axis=0, tiled=True),
        lax.all_to_all(label_send, "col", split_axis=0, concat_axis=0, tiled=True),
    )
    arrived = arrived.reshape(total_slots, block_size, block_size * block_size)
    arrived_labels = arrived_labels.astype(jnp.int32).reshape(total_slots, 4)
    first_in = arrived_labels[:, 0]
    slot_in = arrived_labels[:, 1]
    second_in = arrived_labels[:, 2]
    flag_in = arrived_labels[:, 3]
    picking = (
        (slot_in[:, None] == jnp.arange(owned_slots, dtype=jnp.int32)[None, :])
        & (flag_in[:, None] > 0)
    ).astype(jnp.bfloat16)
    chosen = jnp.einsum("es,sqp->eqp", picking, metric, preferred_element_type=jnp.float32).astype(
        jnp.bfloat16
    )
    applied = jnp.einsum(
        "eqp,eqx->epx", chosen, arrived, preferred_element_type=jnp.float32
    ).astype(jnp.bfloat16)
    kept = jnp.where(pattern[:, None] > 0, density_panel, jnp.zeros_like(density_panel))
    panel_all = lax.all_gather(kept, ("row", "col"), axis=0, tiled=True)
    panel_all = panel_all.reshape(-1, block_size, panel_width)
    group_size = 4
    group_count = total_slots // group_size
    pair_count = owned_slots * MB
    pair_keys = slot_in * MB + first_in
    anchor = jnp.zeros((), jnp.int32)

    def accumulate(running, inputs_now):
        blocks, second, keyed = inputs_now
        for member in range(group_size):
            flat = blocks[member].reshape(block_size * block_size, block_size)
            contrib = jnp.dot(flat, panel_all[second[member]], preferred_element_type=jnp.float32)
            corner = (keyed[member], anchor, anchor, anchor)
            current = lax.dynamic_slice(running, corner, (1, block_size, block_size, panel_width))
            updated = current + contrib.reshape(1, block_size, block_size, panel_width)
            running = lax.dynamic_update_slice(running, updated, corner)
        return (running, None)

    empty_sum = jnp.zeros((pair_count, block_size, block_size, panel_width), jnp.float32)
    grouped = (
        applied.reshape(group_count, group_size, block_size, block_size * block_size),
        second_in.reshape(group_count, group_size),
        pair_keys.reshape(group_count, group_size),
    )
    filled, _ = lax.scan(accumulate, empty_sum, grouped)
    rounded = filled.astype(jnp.bfloat16).reshape(
        owned_slots, MB, block_size, block_size, panel_width
    )
    local_tile = jnp.einsum(
        "jupmo,jvpno->umvn", rounded, rounded, preferred_element_type=jnp.float32
    )
    local_tile = local_tile.reshape(MB * block_size, MB * block_size) * (
        1.0 / (all_slots * block_size * panel_width)
    )
    summed = lax.psum(local_tile, "col")
    share_rows = summed.shape[0] // columns
    result_rows = lax.dynamic_slice_in_dim(
        summed, lax.axis_index("col") * share_rows, share_rows, 0
    )
    return result_rows


def solution(mesh):
    placed = (
        P(("row", "col"), None, None),
        P(("row", "col"), None),
        P(),
        P("col", None, None),
        P(("row", "col"), None),
        P(("row", "col")),
    )
    return jax.shard_map(
        on_device, mesh=mesh, in_specs=placed, out_specs=P(("row", "col"), None), check_vma=False
    )
```

profile of v0, /device:TPU:0, one launch (start us, length us, event | category | flops | bytes accessed | tf_op | source)
XLA Modules:
  0.0 590.8 jit_solution(5425671029016775812)
XLA Ops:
  9.4 7.3 %all-to-all-start = ((bf16[8,2,4]{2,1,0:T(2,128)(2,1)}), bf16[8,2,4]{2,1,0:T(2,128)(2,1)S(1)}, u32[]{:S(2)}, u32[]{:S(2)}) async-start(bf16[8,2,4]{2,1,0:T(2,128)(2,1)} %bitcast.22), calls=%async_computation | async-start | bytes 8192 | tf_op jit(solution)/shard_map/all_to_all | solution.py:43
  16.7 7.2 %pad.4 = bf16[16,64,4096]{2,1,0:T(8,128)(2,1)} pad(bf16[12,64,4096]{2,1,0:T(8,128)(2,1)} %param.8, bf16[]{:T(256)} %constant.62.clone.1), padding=0_4x0_0x0_0 | pad | bytes 14680066
  23.8 11.2 %copy.17 = bf16[2,8,64,4096]{3,1,2,0:T(8,128)(2,1)} copy(bf16[2,8,64,4096]{3,2,1,0:T(8,128)(2,1)} %bitcast.130) | data formatting | bytes 16777216
  35.0 6.9 %convolution_convert_fusion = bf16[16,262144]{1,0:T(8,128)(2,1)} fusion(bf16[12,262144]{1,0:T(8,128)(2,1)} %bitcast.127, s32[12]{0:T(128)S(1)} %multiply_add_fusion), kind=kOutput, calls=%fused_computation.26 | convolution fusion | flops 104857792 | bytes 14680112 | tf_op jit(solution)/shard_map/dot_general | solution.py:32
  41.9 11.2 %copy.18 = bf16[2,8,64,4096]{3,2,1,0:T(8,128)(2,1)} copy(bf16[2,8,64,4096]{3,1,2,0:T(8,128)(2,1)} %bitcast.128) | data formatting | bytes 16777216
  53.1 6.1 %all-to-all-start.1 = ((bf16[8,2,64,4096]{3,2,1,0:T(8,128)(2,1)}), bf16[8,2,64,4096]{3,2,1,0:T(8,128)(2,1)}, u32[]{:S(2)}, u32[]{:S(2)}) async-start(bf16[8,2,64,4096]{3,2,1,0:T(8,128)(2,1)} %bitcast.129), calls=%async_computation.1 | async-start | bytes 16777216 | tf_op jit(solution)/shard_map/all_to_all | solution.py:42
  59.4 245.5 %all_gather.3 = bf16[2048,128]{1,0:T(8,128)(2,1)} all-gather(bf16[64,128]{1,0:T(8,128)(2,1)S(1)} %broadcast_select_fusion), channel_id=1, replica_groups=mesh['row'=4,'col'=8] {'row','col'}, dimensions={0}, use_global_device_ids=true | all-gather | bytes 540672 | tf_op jit(solution)/shard_map/all_gather | solution.py:62
  305.8 9.0 %convolution_convert_fusion.1 = bf16[16,64,4096]{2,1,0:T(8,128)(2,1)} fusion(bf16[16,64,4096]{2,1,0:T(8,128)(2,1)} %bitcast.26, bf16[16,64,64]{2,0,1:T(8,128)(2,1)S(1)} %convolution_convert_fusion.2), kind=kOutput, calls=%fused_computation.27 | convolution fusion | flops 541065216 | bytes 16908288 | tf_op jit(solution)/shard_map/eqp,eqx->epx/dot_general | solution.py:58
  314.8 11.2 %broadcast_in_dim.58 = f32[16,64,64,128]{3,2,1,0:T(8,128)} broadcast(f32[]{:T(128)} %constant.56.clone.1), dimensions={} | broadcast | bytes 33554436 | tf_op jit(solution)/shard_map/broadcast_in_dim | solution.py:81
  326.0 143.0 %while.10 = (s32[]{:T(128)}, f32[16,64,64,128]{3,2,1,0:T(8,128)}, s32[4,4]{1,0:T(4,128)S(1)}, bf16[4,4,64,4096]{3,2,1,0:T(8,128)(2,1)}, s32[4,4]{1,0:T(4,128)S(1...) while((s32[]{:T(128)}, f32[16,64,64,128]{3,2,1,0:T(8,128)}, ...), condition=%wide.region_4.5_spmd, body=%wide.region_3.4_spmd.sunk | while | flops 270532608 | bytes 27329120 | solution.py:87
  330.9 1.7 constant_dynamic-slice_fusion.10
  332.6 1.1 reshape.216
  333.7 3.4 fusion.63
  340.5 1.1 reshape.217
  341.6 3.4 fusion.64
  349.0 1.1 reshape.218
  350.2 3.4 fusion.65
  358.5 3.3 fusion.66
  366.7 1.7 constant_dynamic-slice_fusion.10
  368.4 1.1 reshape.216
  369.5 3.4 fusion.63
  376.2 1.1 reshape.217
  377.4 3.4 fusion.64
  384.8 1.1 reshape.218
  385.9 3.4 fusion.65
  393.1 1.1 reshape.219
  394.2 3.4 fusion.66
  402.5 1.7 constant_dynamic-slice_fusion.10
  404.1 1.1 reshape.216
  405.3 3.4 fusion.63
  412.0 1.1 reshape.217
  413.1 3.4 fusion.64
  420.6 1.1 reshape.218
  421.7 3.4 fusion.65
  429.9 3.3 fusion.66
  438.1 1.7 constant_dynamic-slice_fusion.10
  440.9 3.4 fusion.63
  447.7 1.1 reshape.217
  448.8 3.4 fusion.64
  456.2 1.1 reshape.218
  457.4 3.4 fusion.65
  464.5 1.1 reshape.219
  465.6 3.4 fusion.66
  469.0 12.8 %convert_element_type.31 = bf16[16,64,64,128]{3,2,1,0:T(8,128)(2,1)S(1)} convert(f32[16,64,64,128]{3,2,1,0:T(8,128)} %get-tuple-element.37) | non-fusion elementwise | flops 8388608 | bytes 50331648 | tf_op jit(solution)/shard_map/convert_element_type | solution.py:88
  481.8 7.0 %copy.15 = bf16[8,64,2,128,64]{3,1,0,4,2:T(8,128)(2,1)} copy(bf16[8,64,2,128,64]{3,1,4,0,2:T(8,128)(2,1)S(1)} %bitcast.126) | data formatting | bytes 33554432 | tf_op jit(solution)/shard_map/jupmo,jvpno->umvn/dot_general | solution.py:91
  488.9 18.0 %fusion.16 = f32[512,512]{1,0:T(8,128)} fusion(bf16[512,2,128,64]{2,0,3,1:T(8,128)(2,1)} %bitcast.131), kind=kOutput, calls=%fused_computation.29 | convolution fusion | flops 8590196736 | bytes 17825792 | tf_op jit(solution)/shard_map/jupmo,jvpno->umvn/dot_general | solution.py:91
  506.9 75.4 %all-reduce.2.cloned.1.call-done = f32[512,512]{1,0:T(8,128)} async-done(((f32[512,512]{1,0:T(8,128)}), f32[512,512]{1,0:T(8,128)}) %all-reduce.2.cloned.1.call-update) | async-done | bytes 1048592 | tf_op jit(solution)/shard_map/psum | solution.py:97
  582.4 1.6 constant_dynamic-slice_fusion.6
  (48 shorter events, 12.4 us)
Async XLA Ops:
  6.5 299.0 %copy-start = (bf16[2,64,64]{2,1,0:T(8,128)(2,1)S(1)}, bf16[2,64,64]{2,1,0:T(8,128)(2,1)}, u32[]{:S(2)}) copy-start(bf16[2,64,64]{2,1,0:T(8,128)(2,1)} %param.11) | copy-start | bytes 49156
  9.4 43.7 %all-to-all-start = ((bf16[8,2,4]{2,1,0:T(2,128)(2,1)}), bf16[8,2,4]{2,1,0:T(2,128)(2,1)S(1)}, u32[]{:S(2)}, u32[]{:S(2)}) async-start(bf16[8,2,4]{2,1,0:T(2,128)(2,1)} %bitcast.22), calls=%async_computation | async-start | bytes 8192 | tf_op jit(solution)/shard_map/all_to_all | solution.py:43
  53.1 6.2 %copy-start.3 = (s32[64]{0:T(128)S(1)}, s32[64]{0:T(128)}, u32[]{:S(2)}) copy-start(s32[64]{0:T(128)} %param.13) | copy-start | bytes 772
  53.1 6.2 %copy-start.2 = (bf16[64,128]{1,0:T(8,128)(2,1)S(1)}, bf16[64,128]{1,0:T(8,128)(2,1)}, u32[]{:S(2)}) copy-start(bf16[64,128]{1,0:T(8,128)(2,1)} %param.12) | copy-start | bytes 49156
  53.1 252.7 %all-to-all-start.1 = ((bf16[8,2,64,4096]{3,2,1,0:T(8,128)(2,1)}), bf16[8,2,64,4096]{3,2,1,0:T(8,128)(2,1)}, u32[]{:S(2)}, u32[]{:S(2)}) async-start(bf16[8,2,64,4096]{3,2,1,0:T(8,128)(2,1)} %bitcast.129), calls=%async_computation.1 | async-start | bytes 16777216 | tf_op jit(solution)/shard_map/all_to_all | solution.py:42
  59.3 523.1 %all-reduce.2.cloned.1.call-start = ((), (), s32[]{:S(2)}) async-start(), calls=%async_computation.2 | async-start | bytes 2097152 | tf_op jit(solution)/shard_map/psum | solution.py:97
  488.9 95.1 %copy-start.1 = (bf16[2,64,64]{2,1,0:T(8,128)(2,1)S(1)}, bf16[2,64,64]{2,1,0:T(8,128)(2,1)}, u32[]{:S(2)}) copy-start(bf16[2,64,64]{2,1,0:T(8,128)(2,1)} %param.11) | copy-start | bytes 49156
Sparse Core Ops, SparseCore 0:
  507.1 75.2 all-reduce.1
where the time goes:
time: 593 us; the launch traced here: 591 us
  blocking collectives  246 us (41%)
  matrix products  88.2 us (15%)
  local copies, waits for them, and re-layouts  80.2 us (14%)
  waiting for transfers between devices  75.4 us (13%)
  loops' own time  59.1 us (10%)
  other arithmetic  15.3 us (3%)
  starting transfers between devices  13.5 us (2%)
  between operations  13.5 us (2%)
    all_gather x1, blocking collectives, on_device(): panel_all = lax.all_gather(kept, ('row', 'col'), axis=0, tiled=True)  246 us
    psum x1, waiting for transfers between devices, on_device(): summed = lax.psum(local_tile, 'col')  75.4 us
    another operation x1, loops' own time, on_device(): filled, _ = lax.scan(accumulate, empty_sum, grouped)  59.1 us
    dot_general x16, matrix products, accumulate(): jnp.dot(flat, panel_all[second[member]], preferred_element_type=jnp.float32)  54 us
    unnamed x11, local copies, waits for them, and re-layouts  29.5 us
    dot_general x1, matrix products, on_device(): jnp.einsum('jupmo,jvpno->umvn', rounded, rounded, preferred_element_type=...  18 us
    another operation x16, local copies, waits for them, and re-layouts  18 us
    convert_element_type x1, other arithmetic, on_device(): filled.astype(jnp.bfloat16)  12.8 us
  transfers between devices with their start and end apart: 3, of which 1 were waited for; matrix products, arithmetic and copies ran while one was open for 6% of the time, Pallas kernels for 0%

commit v1 on v0

--- a/solution.py
+++ b/solution.py
@@ -94,7 +94,7 @@
     local_tile = local_tile.reshape(MB * block_size, MB * block_size) * (
         1.0 / (all_slots * block_size * panel_width)
     )
-    summed = lax.psum(local_tile, "col")
+    summed = jnp.sum(lax.all_gather(local_tile, "col"), axis=0)
     share_rows = summed.shape[0] // columns
     result_rows = lax.dynamic_slice_in_dim(
         summed, lax.axis_index("col") * share_rows, share_rows, 0

time: 593 us -> 643 us (1.084)
  waiting for transfers between devices: 75.4 us -> 122 us
    all_gather x0 -> x1, waiting for transfers between devices: none -> 122 us  [on_device(): summed = jnp.sum(lax.all_gather(local_tile, 'col'), axis=0)]
    psum x1 -> x0, waiting for transfers between devices: 75.4 us -> none  [on_device(): summed = lax.psum(local_tile, 'col')]
where the time goes in v1:
time: 643 us; the launch traced here: 641 us
  blocking collectives  246 us (38%)
  waiting for transfers between devices  122 us (19%)
  matrix products  88.2 us (14%)
  local copies, waits for them, and re-layouts  79.3 us (12%)
  loops' own time  59.1 us (9%)
  other arithmetic  19.8 us (3%)
  starting transfers between devices  13.5 us (2%)
  between operations  13.5 us (2%)
    all_gather x1, blocking collectives, on_device(): panel_all = lax.all_gather(kept, ('row', 'col'), axis=0, tiled=True)  246 us
    all_gather x1, waiting for transfers between devices, on_device(): summed = jnp.sum(lax.all_gather(local_tile, 'col'), axis=0)  122 us
    another operation x1, loops' own time, on_device(): filled, _ = lax.scan(accumulate, empty_sum, grouped)  59.1 us
    dot_general x16, matrix products, accumulate(): jnp.dot(flat, panel_all[second[member]], preferred_element_type=jnp.float32)  54 us
    unnamed x11, local copies, waits for them, and re-layouts  29.5 us
    dot_general x1, matrix products, on_device(): jnp.einsum('jupmo,jvpno->umvn', rounded, rounded, preferred_element_type=...  18 us
    another operation x16, local copies, waits for them, and re-layouts  18 us
  transfers between devices with their start and end apart: 3, of which 1 were waited for; matrix products, arithmetic and copies ran while one was open for 6% of the time, Pallas kernels for 0%

profile of v1, /device:TPU:0, one launch (start us, length us, event | category | flops | bytes accessed | tf_op | source)
XLA Modules:
  0.0 640.5 jit_solution(17182884477582610609)
XLA Ops:
  9.4 7.3 %all-to-all-start = ((bf16[8,2,4]{2,1,0:T(2,128)(2,1)}), bf16[8,2,4]{2,1,0:T(2,128)(2,1)S(1)}, u32[]{:S(2)}, u32[]{:S(2)}) async-start(bf16[8,2,4]{2,1,0:T(2,128)(2,1)} %bitcast.22), calls=%async_computation | async-start | bytes 8192 | tf_op jit(solution)/shard_map/all_to_all | solution.py:43
  16.7 7.2 %pad.4 = bf16[16,64,4096]{2,1,0:T(8,128)(2,1)} pad(bf16[12,64,4096]{2,1,0:T(8,128)(2,1)} %param.8, bf16[]{:T(256)} %constant.63.clone.1), padding=0_4x0_0x0_0 | pad | bytes 14680066
  23.8 11.2 %copy.17 = bf16[2,8,64,4096]{3,1,2,0:T(8,128)(2,1)} copy(bf16[2,8,64,4096]{3,2,1,0:T(8,128)(2,1)} %bitcast.131) | data formatting | bytes 16777216
  35.0 6.9 %convolution_convert_fusion = bf16[16,262144]{1,0:T(8,128)(2,1)} fusion(bf16[12,262144]{1,0:T(8,128)(2,1)} %bitcast.128, s32[12]{0:T(128)S(1)} %multiply_add_fusion), kind=kOutput, calls=%fused_computation.26 | convolution fusion | flops 104857792 | bytes 14680112 | tf_op jit(solution)/shard_map/dot_general | solution.py:32
  41.9 11.2 %copy.18 = bf16[2,8,64,4096]{3,2,1,0:T(8,128)(2,1)} copy(bf16[2,8,64,4096]{3,1,2,0:T(8,128)(2,1)} %bitcast.129) | data formatting | bytes 16777216
  53.1 6.1 all-to-all-start.1
  59.4 245.5 %all_gather.9 = bf16[2048,128]{1,0:T(8,128)(2,1)} all-gather(bf16[64,128]{1,0:T(8,128)(2,1)S(1)} %broadcast_select_fusion), channel_id=1, replica_groups=mesh['row'=4,'col'=8] {'row','col'}, dimensions={0}, use_global_device_ids=true | all-gather | bytes 540672 | tf_op jit(solution)/shard_map/all_gather | solution.py:62
  305.8 9.0 %convolution_convert_fusion.1 = bf16[16,64,4096]{2,1,0:T(8,128)(2,1)} fusion(bf16[16,64,4096]{2,1,0:T(8,128)(2,1)} %bitcast.26, bf16[16,64,64]{2,0,1:T(8,128)(2,1)S(1)} %convolution_convert_fusion.2), kind=kOutput, calls=%fused_computation.27 | convolution fusion | flops 541065216 | bytes 16908288 | tf_op jit(solution)/shard_map/eqp,eqx->epx/dot_general | solution.py:58
  314.8 11.2 %broadcast_in_dim.58 = f32[16,64,64,128]{3,2,1,0:T(8,128)} broadcast(f32[]{:T(128)} %constant.39.clone.1), dimensions={} | broadcast | bytes 33554436 | tf_op jit(solution)/shard_map/broadcast_in_dim | solution.py:81
  326.0 143.0 %while.10 = (s32[]{:T(128)}, f32[16,64,64,128]{3,2,1,0:T(8,128)}, s32[4,4]{1,0:T(4,128)S(1)}, bf16[4,4,64,4096]{3,2,1,0:T(8,128)(2,1)}, s32[4,4]{1,0:T(4,128)S(1...) while((s32[]{:T(128)}, f32[16,64,64,128]{3,2,1,0:T(8,128)}, ...), condition=%wide.region_4.5_spmd, body=%wide.region_3.4_spmd.sunk | while | flops 270532608 | bytes 27329120 | solution.py:87
  330.9 1.7 constant_dynamic-slice_fusion.10
  332.6 1.1 reshape.217
  333.7 3.4 fusion.63
  340.5 1.1 reshape.218
  341.6 3.4 fusion.64
  349.0 1.1 reshape.219
  350.2 3.4 fusion.65
  358.5 3.3 fusion.66
  366.7 1.7 constant_dynamic-slice_fusion.10
  368.4 1.1 reshape.217
  369.5 3.4 fusion.63
  376.2 1.1 reshape.218
  377.4 3.4 fusion.64
  384.8 1.1 reshape.219
  385.9 3.4 fusion.65
  393.1 1.1 reshape.220
  394.2 3.4 fusion.66
  402.5 1.7 constant_dynamic-slice_fusion.10
  404.1 1.1 reshape.217
  405.3 3.4 fusion.63
  412.0 1.1 reshape.218
  413.1 3.4 fusion.64
  420.6 1.1 reshape.219
  421.7 3.4 fusion.65
  429.9 3.3 fusion.66
  438.1 1.7 constant_dynamic-slice_fusion.10
  440.9 3.4 fusion.63
  447.7 1.1 reshape.218
  448.8 3.4 fusion.64
  456.2 1.1 reshape.219
  457.4 3.4 fusion.65
  464.5 1.1 reshape.220
  465.6 3.4 fusion.66
  469.0 12.8 %convert_element_type.31 = bf16[16,64,64,128]{3,2,1,0:T(8,128)(2,1)S(1)} convert(f32[16,64,64,128]{3,2,1,0:T(8,128)} %get-tuple-element.37) | non-fusion elementwise | flops 8388608 | bytes 50331648 | tf_op jit(solution)/shard_map/convert_element_type | solution.py:88
  481.8 7.0 %copy.15 = bf16[8,64,2,128,64]{3,1,0,4,2:T(8,128)(2,1)} copy(bf16[8,64,2,128,64]{3,1,4,0,2:T(8,128)(2,1)S(1)} %bitcast.127) | data formatting | bytes 33554432 | tf_op jit(solution)/shard_map/jupmo,jvpno->umvn/dot_general | solution.py:91
  488.9 18.0 %fusion.16 = f32[512,512]{1,0:T(8,128)} fusion(bf16[512,2,128,64]{2,0,3,1:T(8,128)(2,1)} %bitcast.132), kind=kOutput, calls=%fused_computation.29 | convolution fusion | flops 8590196736 | bytes 17825792 | tf_op jit(solution)/shard_map/jupmo,jvpno->umvn/dot_general | solution.py:91
  506.9 121.6 %all-gather.3.cloned.1.call-done = f32[4096,512]{1,0:T(8,128)} async-done(((f32[512,512]{1,0:T(8,128)}), f32[4096,512]{1,0:T(8,128)}) %all-gather.3.cloned.1.call-update) | async-done | bytes 8388624 | tf_op jit(solution)/shard_map/all_gather | solution.py:97
  628.5 4.5 reduce_sum.42
  (49 shorter events, 13.1 us)
Async XLA Ops:
  6.5 299.0 %copy-start = (bf16[2,64,64]{2,1,0:T(8,128)(2,1)S(1)}, bf16[2,64,64]{2,1,0:T(8,128)(2,1)}, u32[]{:S(2)}) copy-start(bf16[2,64,64]{2,1,0:T(8,128)(2,1)} %param.11) | copy-start | bytes 49156
  9.4 43.7 %all-to-all-start = ((bf16[8,2,4]{2,1,0:T(2,128)(2,1)}), bf16[8,2,4]{2,1,0:T(2,128)(2,1)S(1)}, u32[]{:S(2)}, u32[]{:S(2)}) async-start(bf16[8,2,4]{2,1,0:T(2,128)(2,1)} %bitcast.22), calls=%async_computation | async-start | bytes 8192 | tf_op jit(solution)/shard_map/all_to_all | solution.py:43
  53.1 6.2 copy-start.3
  53.1 6.2 copy-start.2
  53.1 252.7 %all-to-all-start.1 = ((bf16[8,2,64,4096]{3,2,1,0:T(8,128)(2,1)}), bf16[8,2,64,4096]{3,2,1,0:T(8,128)(2,1)}, u32[]{:S(2)}, u32[]{:S(2)}) async-start(bf16[8,2,64,4096]{3,2,1,0:T(8,128)(2,1)} %bitcast.130), calls=%async_computation.1 | async-start | bytes 16777216 | tf_op jit(solution)/shard_map/all_to_all | solution.py:42
  59.3 569.2 %all-gather.3.cloned.1.call-start = ((), (), s32[]{:S(2)}) async-start(), calls=%async_computation.2 | async-start | bytes 9437184 | tf_op jit(solution)/shard_map/all_gather | solution.py:97
  488.9 144.8 %copy-start.1 = (bf16[2,64,64]{2,1,0:T(8,128)(2,1)S(1)}, bf16[2,64,64]{2,1,0:T(8,128)(2,1)}, u32[]{:S(2)}) copy-start(bf16[2,64,64]{2,1,0:T(8,128)(2,1)} %param.11) | copy-start | bytes 49156
Sparse Core Ops, SparseCore 0:
  507.1 121.4 all-gather.2
